TPU v7x, 256 devices: a whole 4x4x8 slice. The times are simulated.
256 devices in a mesh: gz: 8 (over x, core), gx: 32 (over z, y).
Axes of the slice: x: 4, y: 4, z: 8, core: 2. Of those that a mesh axis runs over, the one named last changes fastest.
Arguments:
- volume: float32 [256, 512, 256], P('gz', 'gx')
- measured: float32 [2, 256, 2048], P(None, 'gz')
- weight_blocks: bfloat16 [64, 128, 128], replicated, may hold values from 0 to 2
- view_order: int32 [2], replicated, may hold values from 0 to 1, each once
- tile_voxel: int32 [2, 8, 16384], P(None, 'gz', 'gx'), may hold values from 0 to 1023
- tile_column: int32 [2, 8, 16384], P(None, 'gz', 'gx'), may hold values from 0 to 15
- tile_block: int32 [2, 8, 16384], P(None, 'gz', 'gx'), may hold values from 0 to 63
- entry_count: int32 [2, 8, 32], P(None, 'gz', 'gx'), may hold values from 1 to 512, as said below
Outputs:
- volume_out: float32 [256, 512, 256], P('gz', 'gx')
Inputs may be any that keep to these rules, and one draw needn't show every extreme that they name: Entries of block (a, c) of view v at or past entry_count[v, a, c] are not used; in every view some block has 512 live entries.
All inputs are finite; a program needn't handle non-finite values.
Results may differ from a plain program's by a relative error of at most 0.0027.
Values may be sent and summed in bfloat16 or wider, within the bound.
A program may use at most 64 MiB of HBM per device.

v0:
```python
import jax
import jax.numpy as jnp
from jax import lax
from jax.sharding import PartitionSpec as P

TV_STEPS = 4
smooth_floor = 0.01
step_gain = 0.25
norm_floor = 1e-06
group_rows = 128


def padded_2(cells, sides, width):
    for axis, dim in sides:
        count = lax.axis_size(axis)
        ends = count - 1
        head = lax.slice_in_dim(cells, 0, width, axis=dim)
        tail = lax.slice_in_dim(cells, cells.shape[dim] - width, cells.shape[dim], axis=dim)
        cells = jnp.concatenate(
            [
                lax.ppermute(tail, axis, [(i, (i + 1) % count) for i in range(ends)]),
                cells,
                lax.ppermute(head, axis, [((i + 1) % count, i) for i in range(ends)]),
            ],
            axis=dim,
        )
    return cells


def tv_grad(padded):
    base_cells = padded[:-1, :-1, :-1]
    diff_z = padded[1:, :-1, :-1] - base_cells
    diff_x = padded[:-1, 1:, :-1] - base_cells
    diff_y = padded[:-1, :-1, 1:] - base_cells
    inverse = lax.rsqrt(diff_z * diff_z + diff_x * diff_x + diff_y * diff_y + smooth_floor)
    flow_z = diff_z * inverse
    flow_x = diff_x * inverse
    flow_y = diff_y * inverse
    flow_all = flow_z + flow_x + flow_y
    return flow_z[:-1, 1:, 1:] + flow_x[1:, :-1, 1:] + flow_y[1:, 1:, :-1] - flow_all[1:, 1:, 1:]


def pad_depth(field):
    return jnp.pad(field, ((0, 0), (0, 0), (1, 1)))


def body(
    volume, measured, weight_blocks, view_order, tile_voxel, tile_column, tile_block, entry_count
):
    depth_z, depth_x, depth_y = volume.shape
    tiles_y = depth_y // group_rows
    tiles_u = measured.shape[2] // group_rows
    slab_tiles = depth_z * tiles_u
    plane_tiles = depth_x * tiles_y
    row_weight = jnp.sum(weight_blocks, axis=2, dtype=jnp.float32)
    col_weight = jnp.sum(weight_blocks, axis=1, dtype=jnp.float32)
    offsets = jnp.arange(group_rows, dtype=jnp.int32)
    current = volume
    for turn_index in range(view_order.shape[0]):
        view_index = view_order[turn_index]
        voxel_list = lax.dynamic_index_in_dim(tile_voxel, view_index, 0, keepdims=False)[0]
        column_list = lax.dynamic_index_in_dim(tile_column, view_index, 0, keepdims=False)[0]
        block_list = lax.dynamic_index_in_dim(tile_block, view_index, 0, keepdims=False)[0]
        live_count = lax.dynamic_index_in_dim(entry_count, view_index, 0, keepdims=False)[0, 0]
        rounds = (live_count + group_rows - 1) // group_rows
        voxel_tiles = current.astype(jnp.bfloat16).reshape(-1, group_rows)

        def gather_group(index):
            begin = index * group_rows
            voxels = lax.dynamic_slice_in_dim(voxel_list, begin, group_rows)
            columns = lax.dynamic_slice_in_dim(column_list, begin, group_rows)
            chosen = lax.dynamic_slice_in_dim(block_list, begin, group_rows)
            weight = (begin + offsets < live_count).astype(jnp.float32)[:, None]
            detector = voxels // plane_tiles * tiles_u + columns
            return (voxels, detector, chosen, weight)

        def forward(index, carry):
            projection, ray_sum = carry
            voxels, detector, chosen, weight = gather_group(index)
            product = jnp.einsum(
                "ejk,ek->ej",
                weight_blocks[chosen],
                voxel_tiles[voxels],
                preferred_element_type=jnp.float32,
            )
            return (
                projection.at[detector].add(product * weight),
                ray_sum.at[detector].add(row_weight[chosen] * weight),
            )

        empty = jnp.zeros((slab_tiles, group_rows), jnp.float32)
        projection, ray_sum = lax.fori_loop(0, rounds, forward, (empty, empty))
        target = lax.dynamic_index_in_dim(measured, view_index, 0, keepdims=False).reshape(
            slab_tiles, group_rows
        )
        projection, ray_sum = (
            lax.psum(projection.astype(jnp.bfloat16), "gx").astype(jnp.float32),
            lax.psum(ray_sum.astype(jnp.bfloat16), "gx").astype(jnp.float32),
        )
        residual = ((target - projection) / (ray_sum + 1.0)).astype(jnp.bfloat16)

        def backward(index, carry):
            change, voxel_sum = carry
            voxels, detector, chosen, weight = gather_group(index)
            product = jnp.einsum(
                "ejk,ej->ek",
                weight_blocks[chosen],
                residual[detector],
                preferred_element_type=jnp.float32,
            )
            return (
                change.at[voxels].add(product * weight),
                voxel_sum.at[voxels].add(col_weight[chosen] * weight),
            )

        blank = jnp.zeros((voxel_tiles.shape[0], group_rows), jnp.float32)
        change, voxel_sum = lax.fori_loop(0, rounds, backward, (blank, blank))
        current = current + (change / (voxel_sum + 1.0)).reshape(current.shape)
    art_volume = jnp.maximum(current, 0.0)
    difference = art_volume - volume
    change_part = jnp.sum(difference * difference)
    change_total = None
    change_total = lax.psum(change_part, ("gz", "gx"))
    smooth = art_volume
    for sweep_index in range(TV_STEPS):
        padded = padded_2(smooth, (("gz", 0), ("gx", 1)), 1)
        slope = tv_grad(pad_depth(padded))
        slope_part = jnp.sum(slope * slope)
        if sweep_index == 0:
            slope_total = lax.psum(slope_part, ("gz", "gx"))
        else:
            slope_total = lax.psum(slope_part, ("gz", "gx"))
        change_total, scale_now = (
            change_total,
            step_gain * jnp.sqrt(change_total) / jnp.sqrt(slope_total + norm_floor),
        )
        smooth = smooth - scale_now * slope
    return smooth


def solution(mesh):
    return jax.shard_map(
        body,
        mesh=mesh,
        in_specs=(
            P("gz", "gx", None),
            P(None, "gz", None),
            P(),
            P(),
            P(None, "gz", "gx"),
            P(None, "gz", "gx"),
            P(None, "gz", "gx"),
            P(None, "gz", "gx"),
        ),
        out_specs=P("gz", "gx", None),
        check_vma=False,
    )
```

profile of v0, /device:TPU:1, one launch (start us, length us, event | category | flops | bytes accessed | tf_op | source)
XLA Modules:
  0.0 943.3 jit_solution(2549535672975663778)
XLA Ops:
  17.6 13.5 %while.60 = (s32[]{:T(128)}, f32[512,128]{1,0:T(8,128)S(1)}, f32[512,128]{1,0:T(8,128)}, s32[]{:T(128)}, s32[512]{0:T(512)S(1)}, /*index=5*/s32[512]{0:T(512)S(1...) while((s32[]{:T(128)}, f32[512,128]{1,0:T(8,128)S(1)}, ...), condition=%wide.region_4.5_spmd.clone, body=%wide.region_1.4_spmd.clone.sunk | while | flops 4265478 | bytes 13388487 | solution.py:92
  17.7 3.0 gather_fusion
  21.5 4.4 fusion.99
  28.1 3.1 scatter_custom_fusion.43
  36.0 180.4 %all-reduce.12.cloned.1.call-done = (bf16[512,128]{1,0:T(8,128)(2,1)}, bf16[512,128]{1,0:T(8,128)(2,1)}) async-done(((bf16[512,128]{1,0:T(8,128)(2,1)}, bf16[512,128]{1,0:T(8,128)(2,1)}), (bf16[512,128]{1,0:T(8,128)(2,1)}, bf16[512,128]{1,0:T(8,128)(2,1)})) %all-reduce.12.cloned.1.call-update) | async-done | bytes 262160 | tf_op jit(solution)/shard_map/psum | solution.py:98
  219.1 14.2 %while.61 = (s32[]{:T(128)}, f32[1024,128]{1,0:T(8,128)}, f32[1024,128]{1,0:T(8,128)}, s32[]{:T(128)}, s32[512]{0:T(512)S(1)}, /*index=5*/s32[512]{0:T(512)S(1)}...) while((s32[]{:T(128)}, f32[1024,128]{1,0:T(8,128)}, ...), condition=%wide.region_11.12_spmd.clone, body=%wide.region_8.11_spmd.clone.sunk | while | flops 4265478 | bytes 13912775 | solution.py:117
  223.0 3.4 fusion.104
  227.0 3.1 scatter_custom_fusion.46
  230.1 3.3 scatter_custom_fusion.47
  241.9 14.9 %while.62 = (s32[]{:T(128)}, f32[512,128]{1,0:T(8,128)}, f32[512,128]{1,0:T(8,128)}, s32[]{:T(128)}, s32[512]{0:T(512)S(1)}, /*index=5*/s32[512]{0:T(512)S(1)}, ...) while((s32[]{:T(128)}, f32[512,128]{1,0:T(8,128)}, ...), condition=%wide.region_15.16_spmd.clone, body=%wide.region_12.15_spmd.clone.sunk | while | flops 4265478 | bytes 13388487 | solution.py:92
  245.7 4.4 fusion.109
  253.7 3.1 scatter_custom_fusion.51
  260.8 227.2 %all-reduce.10.cloned.1.call-done = (bf16[512,128]{1,0:T(8,128)(2,1)}, bf16[512,128]{1,0:T(8,128)(2,1)}) async-done(((bf16[512,128]{1,0:T(8,128)(2,1)}, bf16[512,128]{1,0:T(8,128)(2,1)}), (bf16[512,128]{1,0:T(8,128)(2,1)}, bf16[512,128]{1,0:T(8,128)(2,1)})) %all-reduce.10.cloned.1.call-update) | async-done | bytes 262160 | tf_op jit(solution)/shard_map/psum | solution.py:98
  490.0 12.7 %while.63 = (s32[]{:T(128)}, f32[1024,128]{1,0:T(8,128)S(1)}, f32[1024,128]{1,0:T(8,128)}, s32[]{:T(128)}, s32[512]{0:T(512)S(1)}, /*index=5*/s32[512]{0:T(512)S...) while((s32[]{:T(128)}, f32[1024,128]{1,0:T(8,128)S(1)}, ...), condition=%wide.region_21.22_spmd.clone, body=%wide.region_18.21_spmd.clone.sunk | while | flops 4265478 | bytes 13912775 | solution.py:117
  493.8 3.4 fusion.114
  499.4 3.3 scatter_custom_fusion.55
  504.9 8.1 collective-permute-start
  514.9 3.1 collective-permute-done.1
  521.3 3.4 collective-permute-done.3
  527.9 113.9 %all-reduce.4 = (f32[]{:T(128)}, f32[]{:T(128)}) all-reduce(f32[]{:T(128)} %get-tuple-element.839, f32[]{:T(128)} %get-tuple-element.837), channel_id=1, replica_groups=mesh['gz'=8,'gx'=32] {'gz','gx'}, use_global_device_ids=true, to_apply=%region_23.24 | all-reduce | flops 2 | bytes 16 | tf_op jit(solution)/shard_map/psum | solution.py:123
  643.4 3.5 collective-permute-start.4
  648.9 3.1 collective-permute-done.5
  654.8 3.6 collective-permute-done.7
  661.7 77.6 %psum.69 = f32[]{:T(128)} all-reduce(f32[]{:T(128)} %get-tuple-element.833), channel_id=1, replica_groups=mesh['gz'=8,'gx'=32] {'gz','gx'}, use_global_device_ids=true, to_apply=%region_27.28 | all-reduce | flops 1 | bytes 8 | tf_op jit(solution)/shard_map/psum | solution.py:132
  740.1 3.5 collective-permute-start.8
  745.5 3.1 collective-permute-done.9
  751.6 3.4 collective-permute-done.11
  758.3 78.8 %psum.70 = f32[]{:T(128)} all-reduce(f32[]{:T(128)} %get-tuple-element.829), channel_id=1, replica_groups=mesh['gz'=8,'gx'=32] {'gz','gx'}, use_global_device_ids=true, to_apply=%region_29.30 | all-reduce | flops 1 | bytes 8 | tf_op jit(solution)/shard_map/psum | solution.py:132
  837.8 3.5 collective-permute-start.12
  843.3 3.1 collective-permute-done.13
  849.2 3.6 collective-permute-done.15
  856.0 78.8 %psum.71 = f32[]{:T(128)} all-reduce(f32[]{:T(128)} %get-tuple-element.825), channel_id=1, replica_groups=mesh['gz'=8,'gx'=32] {'gz','gx'}, use_global_device_ids=true, to_apply=%region_31.32 | all-reduce | flops 1 | bytes 8 | tf_op jit(solution)/shard_map/psum | solution.py:132
  (119 shorter events, 84.7 us)
Async XLA Ops:
  6.5 10.1 %copy-start.1 = (f32[32,16,256]{2,1,0:T(8,128)S(1)}, f32[32,16,256]{2,1,0:T(8,128)}, u32[]{:S(2)}) copy-start(f32[32,16,256]{2,1,0:T(8,128)} %param.16) | copy-start | bytes 1572868
  6.5 209.8 %all-reduce.12.cloned.1.call-start = ((), (), s32[]{:S(2)}) async-start(), calls=%async_computation.1 | async-start | bytes 524288 | tf_op jit(solution)/shard_map/psum | solution.py:98
  14.3 2.6 copy-start.3
  14.3 2.6 copy-start.4
  14.3 3.4 copy-start
  33.4 454.6 %all-reduce.10.cloned.1.call-start = ((), (), s32[]{:S(2)}) async-start(), calls=%async_computation | async-start | bytes 524288 | tf_op jit(solution)/shard_map/psum | solution.py:98
  502.7 1.3 copy-start.2
  504.9 10.0 %collective-permute-start = (f32[1,16,256]{2,1,0:T(8,128)S(1)}, f32[1,16,256]{2,1,0:T(8,128)S(1)}, u32[]{:S(2)}, u32[]{:S(2)}) collective-permute-start(f32[1,16,256]{2,1,0:T(8,128)S(1)} %get-tuple-element.879), channel_id=1, source_target_pairs={{0,32},{32,64},{64,96},{96,128},{128,160},{160,192},{192,224},{1,3... | collective-permute-start | bytes 49160 | tf_op jit(solution)/shard_map/ppermute | solution.py:21
  513.0 5.1 collective-permute-start.1
  518.1 3.3 collective-permute-start.2
  520.0 4.7 collective-permute-start.3
  643.4 5.5 collective-permute-start.4
  647.0 5.1 collective-permute-start.5
  652.1 2.7 collective-permute-start.6
  653.5 4.9 collective-permute-start.7
  740.1 5.4 collective-permute-start.8
  743.6 5.1 collective-permute-start.9
  748.7 2.9 collective-permute-start.10
  750.1 4.9 collective-permute-start.11
  837.8 5.4 collective-permute-start.12
  841.3 5.1 collective-permute-start.13
  846.5 2.7 collective-permute-start.14
  847.9 4.9 collective-permute-start.15
Sparse Core Ops, SparseCore 0:
  33.6 182.7 all-reduce.11
  260.1 227.8 all-reduce.9
where the time goes:
time: 946 us; the launch traced here: 943 us
  waiting for transfers between devices  434 us (46%)
  blocking collectives  349 us (37%)
  other arithmetic  55.2 us (6%)
  starting transfers between devices  37.9 us (4%)
  local copies, waits for them, and re-layouts  28.9 us (3%)
  between operations  22.3 us (2%)
  matrix products  15.6 us (2%)
    psum x2, waiting for transfers between devices, body(): lax.psum(ray_sum.astype(jnp.bfloat16), 'gx').astype(jnp.float32)  408 us
    psum x3, blocking collectives, body(): slope_total = lax.psum(slope_part, ('gz', 'gx'))  235 us
    psum x1, blocking collectives, body(): change_total = lax.psum(change_part, ('gz', 'gx'))  114 us
    ppermute x8, waiting for transfers between devices, padded_2(): lax.ppermute(head, axis, [((i + 1) % count, i) for i in range(ends)])  26.5 us
    ppermute x8, starting transfers between devices, padded_2(): lax.ppermute(tail, axis, [(i, (i + 1) % count) for i in range(ends)])  24.8 us
  transfers between devices with their start and end apart: 18, of which 10 were waited for; matrix products, arithmetic and copies ran while one was open for 0% of the time, Pallas kernels for 0%

commit v1 on v0

--- a/solution.py
+++ b/solution.py
@@ -95,7 +95,7 @@
         )
         projection, ray_sum = (
             lax.psum(projection.astype(jnp.bfloat16), "gx").astype(jnp.float32),
-            lax.psum(ray_sum.astype(jnp.bfloat16), "gx").astype(jnp.float32),
+            jnp.sum(lax.all_gather(ray_sum.astype(jnp.bfloat16), "gx"), axis=0).astype(jnp.float32),
         )
         residual = ((target - projection) / (ray_sum + 1.0)).astype(jnp.bfloat16)
 

time: 946 us -> 1100 us (1.16)
  waiting for transfers between devices: 434 us -> 585 us
    all_gather x0 -> x2, waiting for transfers between devices: none -> 283 us  [body(): lax.all_gather(ray_sum.astype(jnp.bfloat16), 'gx')]
    psum x2, waiting for transfers between devices: 408 us -> 275 us  [body(): lax.psum(projection.astype(jnp.bfloat16), 'gx').astype(jnp.float32)]
  transfers between devices with their start and end apart: 18 -> 20, of which waited for: 10 -> 12; matrix products, arithmetic and copies ran while one was open for 0% -> 1% of each run, Pallas kernels for 0% -> 0%
where the time goes in v1:
time: 1100 us
  waiting for transfers between devices  585 us (53%)
  blocking collectives  348 us (32%)
  other arithmetic  60.5 us (6%)
  starting transfers between devices  38.6 us (4%)
  local copies, waits for them, and re-layouts  28.9 us (3%)
  between operations  22.1 us (2%)
  matrix products  15.6 us (1%)
    all_gather x2, waiting for transfers between devices, body(): lax.all_gather(ray_sum.astype(jnp.bfloat16), 'gx')  283 us
    psum x2, waiting for transfers between devices, body(): lax.psum(projection.astype(jnp.bfloat16), 'gx').astype(jnp.float32)  275 us
    psum x3, blocking collectives, body(): slope_total = lax.psum(slope_part, ('gz', 'gx'))  235 us
    psum x1, blocking collectives, body(): change_total = lax.psum(change_part, ('gz', 'gx'))  112 us
    ppermute x8, waiting for transfers between devices, padded_2(): lax.ppermute(head, axis, [((i + 1) % count, i) for i in range(ends)])  26.5 us
    ppermute x8, starting transfers between devices, padded_2(): lax.ppermute(tail, axis, [(i, (i + 1) % count) for i in range(ends)])  25.2 us
  transfers between devices with their start and end apart: 20, of which 12 were waited for; matrix products, arithmetic and copies ran while one was open for 1% of the time, Pallas kernels for 0%

profile of v1, /device:TPU:1, one launch (start us, length us, event | category | flops | bytes accessed | tf_op | source)
XLA Modules:
  0.0 1098.1 jit_solution(14748428521687084278)
XLA Ops:
  17.7 13.4 %while.60 = (s32[]{:T(128)}, f32[512,128]{1,0:T(8,128)S(1)}, f32[512,128]{1,0:T(8,128)}, s32[]{:T(128)}, s32[512]{0:T(512)S(1)}, /*index=5*/s32[512]{0:T(512)S(1...) while((s32[]{:T(128)}, f32[512,128]{1,0:T(8,128)S(1)}, ...), condition=%wide.region_4.5_spmd.clone, body=%wide.region_1.4_spmd.clone.sunk | while | flops 4265478 | bytes 13388487 | solution.py:92
  21.6 4.4 fusion.99
  28.0 3.1 scatter_custom_fusion.43
  36.0 118.7 %all-gather.5.cloned.1.call-done = bf16[16384,128]{1,0:T(8,128)(2,1)} async-done(((bf16[512,128]{1,0:T(8,128)(2,1)}), bf16[16384,128]{1,0:T(8,128)(2,1)}) %all-gather.5.cloned.1.call-update) | async-done | bytes 4194320 | tf_op jit(solution)/shard_map/all_gather | solution.py:98
  157.5 137.6 %all-reduce.8.cloned.1.call-done = bf16[512,128]{1,0:T(8,128)(2,1)} async-done(((bf16[512,128]{1,0:T(8,128)(2,1)}), bf16[512,128]{1,0:T(8,128)(2,1)}) %all-reduce.8.cloned.1.call-update) | async-done | bytes 131088 | tf_op jit(solution)/shard_map/psum | solution.py:97
  297.8 14.1 %while.61 = (s32[]{:T(128)}, f32[1024,128]{1,0:T(8,128)}, f32[1024,128]{1,0:T(8,128)}, s32[]{:T(128)}, s32[512]{0:T(512)S(1)}, /*index=5*/s32[512]{0:T(512)S(1)}...) while((s32[]{:T(128)}, f32[1024,128]{1,0:T(8,128)}, ...), condition=%wide.region_11.12_spmd.clone, body=%wide.region_8.11_spmd.clone.sunk | while | flops 4265478 | bytes 13912775 | solution.py:117
  301.6 3.4 fusion.104
  308.7 3.2 scatter_custom_fusion.47
  320.4 14.9 %while.62 = (s32[]{:T(128)}, f32[512,128]{1,0:T(8,128)}, f32[512,128]{1,0:T(8,128)}, s32[]{:T(128)}, s32[512]{0:T(512)S(1)}, /*index=5*/s32[512]{0:T(512)S(1)}, ...) while((s32[]{:T(128)}, f32[512,128]{1,0:T(8,128)}, ...), condition=%wide.region_15.16_spmd.clone, body=%wide.region_12.15_spmd.clone.sunk | while | flops 4265478 | bytes 13388487 | solution.py:92
  324.3 4.4 fusion.109
  332.3 3.1 scatter_custom_fusion.51
  339.6 164.2 %all-gather.7.cloned.1.call-done = bf16[16384,128]{1,0:T(8,128)(2,1)} async-done(((bf16[512,128]{1,0:T(8,128)(2,1)}), bf16[16384,128]{1,0:T(8,128)(2,1)}) %all-gather.7.cloned.1.call-update) | async-done | bytes 4194320 | tf_op jit(solution)/shard_map/all_gather | solution.py:98
  506.7 137.8 %all-reduce.10.cloned.1.call-done = bf16[512,128]{1,0:T(8,128)(2,1)} async-done(((bf16[512,128]{1,0:T(8,128)(2,1)}), bf16[512,128]{1,0:T(8,128)(2,1)}) %all-reduce.10.cloned.1.call-update) | async-done | bytes 131088 | tf_op jit(solution)/shard_map/psum | solution.py:97
  646.3 12.7 %while.63 = (s32[]{:T(128)}, f32[1024,128]{1,0:T(8,128)S(1)}, f32[1024,128]{1,0:T(8,128)}, s32[]{:T(128)}, s32[512]{0:T(512)S(1)}, /*index=5*/s32[512]{0:T(512)S...) while((s32[]{:T(128)}, f32[1024,128]{1,0:T(8,128)S(1)}, ...), condition=%wide.region_21.22_spmd.clone, body=%wide.region_18.21_spmd.clone.sunk | while | flops 4265478 | bytes 13912775 | solution.py:117
  650.1 3.4 fusion.114
  655.7 3.3 scatter_custom_fusion.55
  661.2 7.4 collective-permute-start
  670.5 3.1 collective-permute-done.1
  673.7 3.1 collective-permute-start.2
  678.1 3.4 collective-permute-done.3
  684.8 112.3 %all-reduce.4 = (f32[]{:T(128)}, f32[]{:T(128)}) all-reduce(f32[]{:T(128)} %get-tuple-element.835, f32[]{:T(128)} %get-tuple-element.833), channel_id=1, replica_groups=mesh['gz'=8,'gx'=32] {'gz','gx'}, use_global_device_ids=true, to_apply=%region_23.24 | all-reduce | flops 2 | bytes 16 | tf_op jit(solution)/shard_map/psum | solution.py:123
  798.6 3.5 collective-permute-start.4
  804.0 3.1 collective-permute-done.5
  809.9 3.6 collective-permute-done.7
  816.8 77.7 %psum.53 = f32[]{:T(128)} all-reduce(f32[]{:T(128)} %get-tuple-element.829), channel_id=1, replica_groups=mesh['gz'=8,'gx'=32] {'gz','gx'}, use_global_device_ids=true, to_apply=%region_27.28 | all-reduce | flops 1 | bytes 8 | tf_op jit(solution)/shard_map/psum | solution.py:132
  895.3 3.5 collective-permute-start.8
  906.6 3.6 collective-permute-done.11
  913.4 78.8 %psum.54 = f32[]{:T(128)} all-reduce(f32[]{:T(128)} %get-tuple-element.825), channel_id=1, replica_groups=mesh['gz'=8,'gx'=32] {'gz','gx'}, use_global_device_ids=true, to_apply=%region_29.30 | all-reduce | flops 1 | bytes 8 | tf_op jit(solution)/shard_map/psum | solution.py:132
  993.0 3.5 collective-permute-start.12
  998.4 3.1 collective-permute-done.13
  1004.3 3.6 collective-permute-done.15
  1011.2 78.8 %psum.55 = f32[]{:T(128)} all-reduce(f32[]{:T(128)} %get-tuple-element.821), channel_id=1, replica_groups=mesh['gz'=8,'gx'=32] {'gz','gx'}, use_global_device_ids=true, to_apply=%region_31.32 | all-reduce | flops 1 | bytes 8 | tf_op jit(solution)/shard_map/psum | solution.py:132
  (129 shorter events, 97.3 us)
Async XLA Ops:
  6.5 10.2 copy-start.1
  6.5 148.2 %all-gather.5.cloned.1.call-start = ((), (), s32[]{:S(2)}) async-start(), calls=%async_computation.2 | async-start | bytes 4325376 | tf_op jit(solution)/shard_map/all_gather | solution.py:98
  14.4 2.6 copy-start.4
  14.4 2.6 copy-start.5
  14.4 3.4 copy-start
  32.7 262.4 %all-reduce.8.cloned.1.call-start = ((), (), s32[]{:S(2)}) async-start(), calls=%async_computation | async-start | bytes 262144 | tf_op jit(solution)/shard_map/psum | solution.py:97
  33.5 470.4 %all-gather.7.cloned.1.call-start = ((), (), s32[]{:S(2)}) async-start(), calls=%async_computation.3 | async-start | bytes 4325376 | tf_op jit(solution)/shard_map/all_gather | solution.py:98
  337.0 307.5 %all-reduce.10.cloned.1.call-start = ((), (), s32[]{:S(2)}) async-start(), calls=%async_computation.1 | async-start | bytes 262144 | tf_op jit(solution)/shard_map/psum | solution.py:97
  503.9 140.6 %copy-start.3 = (f32[512,128]{1,0:T(8,128)S(1)}, f32[512,128]{1,0:T(8,128)}, u32[]{:S(2)}) copy-start(f32[512,128]{1,0:T(8,128)} %reshape.55) | copy-start | bytes 786436
  659.0 1.3 copy-start.2
  661.2 9.3 collective-permute-start
  668.6 5.1 collective-permute-start.1
  673.7 4.4 collective-permute-start.2
  676.8 4.7 collective-permute-start.3
  798.6 5.5 collective-permute-start.4
  802.1 5.1 collective-permute-start.5
  807.2 2.7 collective-permute-start.6
  808.6 4.9 collective-permute-start.7
  895.3 5.6 collective-permute-start.8
  898.7 5.1 collective-permute-start.9
  903.8 2.7 collective-permute-start.10
  905.2 4.9 collective-permute-start.11
  993.0 5.4 collective-permute-start.12
  996.5 5.1 collective-permute-start.13
  1001.6 2.7 collective-permute-start.14
  1003.0 4.9 collective-permute-start.15
Sparse Core Ops, SparseCore 0:
  32.9 121.8 all-gather.4
  158.2 136.8 all-reduce.7
  337.1 166.6 all-gather.6
  507.6 136.8 all-reduce.9
